TPU v7x, 512 devices: a whole 4x8x8 slice. The times are simulated.
512 devices in a mesh: head: 8 (over y), ctx: 16 (over z, core), rep: 4 (over x).
Axes of the slice: x: 4, y: 8, z: 8, core: 2. Of those that a mesh axis runs over, the one named last changes fastest.
Arguments:
- inputs: bfloat16 [4, 8192, 8192], P('rep', 'ctx', 'head'), may hold values from -6 to 6
- b_proj: bfloat16 [4, 8192, 2048], P('rep', 'ctx', 'head'), may hold values from -0.375 to 0.375
- c_proj: bfloat16 [4, 8192, 2048], P('rep', 'ctx', 'head'), may hold values from -0.375 to 0.375
- log_decay: bfloat16 [4, 128, 8192], P('rep', 'head', 'ctx'), may hold values from -1 to 0
- starts: int32 [4, 8192], P('rep', 'ctx'), may hold values 0 or 1
- counts: int32 [4, 16], P('rep', 'ctx'), may hold values from 0 to 512, as said below
- skip_gain: float32 [128], P('head'), may hold values from 0.5 to 1.5
- readout: bfloat16 [8192], P('head'), may hold values from -0.0625 to 0.0625
Outputs:
- ssd_out: bfloat16 [4, 8192, 8192], P('rep', 'ctx', 'head')
- token_scores: float32 [4, 8192], P('rep', 'ctx')
Inputs may be any that keep to these rules, and one draw needn't show every extreme that they name: `counts`: at each ctx index, the two rows 2q and 2q + 1 (q = 0, 1, ...) together hold live slots in exactly 2 spans, counting ceil(count / 256) for each; one of the two holds all of them and the other none.
All inputs are finite; a program needn't handle non-finite values. No bound on the sum of `starts` on one device may be relied on, other than what follows from the above.
Results may differ from a plain program's by a relative error of at most 0.0056.
Values may be sent and summed in bfloat16 or wider, within the bound.
A program may use at most 64 MiB of HBM per device.

v0:
```python
import jax
import jax.numpy as jnp
from jax import lax
from jax.sharding import PartitionSpec as P

SPAN = 256
precise = lax.Precision.HIGHEST


def entering_2(value, axis, join, neutral):
    count, mine = (lax.axis_size(axis), lax.axis_index(axis))
    pieces = jax.tree.map(lambda part: lax.all_gather(part, axis), value)
    total = jax.tree.map(
        lambda part, zero: jnp.full_like(part, 0) + jnp.asarray(zero, part.dtype), value, neutral
    )

    def lap(position, total):
        longer = join(total, jax.tree.map(lambda part: part[position], pieces))
        return jax.tree.map(lambda new, old: jnp.where(position < mine, new, old), longer, total)

    return lax.fori_loop(0, count - 1, lap, total)


def span_basics(span_a, span_s):
    length = span_a.shape[-1]
    reset_positions = jnp.arange(length)
    triangle = (reset_positions[:, None] <= reset_positions[None, :]).astype(jnp.float32)
    cum_decay = jnp.dot(span_a.astype(jnp.float32), triangle, precision=precise)
    doc_index = jnp.dot(span_s.astype(jnp.float32), triangle, precision=precise)
    return (reset_positions, cum_decay, doc_index)


def diag_part(span_x, span_b, span_c, span_a, span_s):
    reset_positions, cum_decay, doc_index = span_basics(span_a, span_s)
    head_count = span_a.shape[0]
    length = span_x.shape[0]
    same_doc = (reset_positions[:, None] >= reset_positions[None, :]) & (
        doc_index[:, None] == doc_index[None, :]
    )
    decay_gaps = cum_decay[:, :, None] - cum_decay[:, None, :]
    decay_mat = jnp.where(same_doc, jnp.exp(jnp.minimum(decay_gaps, 0.0)), 0.0)
    scores = jnp.einsum("in,jn->ij", span_c, span_b, preferred_element_type=jnp.float32)
    weights = (decay_mat * scores[None]).astype(jnp.bfloat16)
    per_head = span_x.reshape(length, head_count, -1)
    diag_out = jnp.einsum("hij,jhp->ihp", weights, per_head, preferred_element_type=jnp.float32)
    return diag_out.astype(jnp.bfloat16).reshape(length, -1)


def state_part(span_x, span_b, span_a, span_s):
    reset_positions, cum_decay, doc_index = span_basics(span_a, span_s)
    head_count = span_a.shape[0]
    length = span_x.shape[0]
    last_cum = cum_decay[:, -1]
    end_keep = jnp.where(
        doc_index[None, :] == doc_index[-1], jnp.exp(last_cum[:, None] - cum_decay), 0.0
    )
    weighted_b = (end_keep[:, :, None] * span_b[None].astype(jnp.float32)).astype(jnp.bfloat16)
    per_head = span_x.reshape(length, head_count, -1)
    span_state = jnp.einsum(
        "hjn,jhp->hpn", weighted_b, per_head, preferred_element_type=jnp.float32
    )
    span_total = jnp.where(doc_index[-1] == 0, jnp.exp(last_cum), 0.0)
    entry_keep = jnp.where(doc_index[None, :] == 0, jnp.exp(cum_decay), 0.0)
    return (span_state, span_total, entry_keep)


def combine_carry(earlier, later):
    return (earlier[0] * later[0], later[0][:, None, None] * earlier[1] + later[1])


def local_diag(span_items):
    return lax.map(lambda one_span: diag_part(*one_span), span_items)


def pass_carry(device_pair, start_pair):
    return entering_2(device_pair, "ctx", combine_carry, start_pair)[1]


def within_outputs(x_blocks, b_blocks, c_blocks, a_blocks, s_blocks):
    return local_diag((x_blocks, b_blocks, c_blocks, a_blocks, s_blocks))


def body(inputs, b_proj, c_proj, log_decay, starts, counts, skip_gain, readout):
    tokens = inputs.shape[1]
    length = SPAN
    blocks = tokens // length
    head_count = log_decay.shape[1]
    live_count = counts[0, 0]
    live_mask = jnp.arange(tokens) < live_count
    masked_x = jnp.where(live_mask[:, None], inputs[0], jnp.zeros((), inputs.dtype))
    masked_a = jnp.where(live_mask[None, :], log_decay[0], jnp.zeros((), log_decay.dtype))
    masked_s = jnp.where(live_mask, starts[0], 0)
    x_blocks = masked_x.reshape(blocks, length, -1)
    b_blocks = b_proj[0].reshape(blocks, length, -1)
    c_blocks = c_proj[0].reshape(blocks, length, -1)
    a_blocks = masked_a.reshape(head_count, blocks, length).transpose(1, 0, 2)
    s_blocks = masked_s.reshape(blocks, length)
    state_all, total_all, entry_all = lax.map(
        lambda one_span: state_part(*one_span), (x_blocks, b_blocks, a_blocks, s_blocks)
    )

    def fold_span(carried, span_items):
        total_now, state_now = span_items
        return ((carried[0] * total_now, total_now[:, None, None] * carried[1] + state_now), None)

    start_pair = (jnp.ones((head_count,), jnp.float32), jnp.zeros(state_all.shape[1:], jnp.float32))
    device_pair, unused_out = lax.scan(fold_span, start_pair, (total_all, state_all))
    diag_all = within_outputs(x_blocks, b_blocks, c_blocks, a_blocks, s_blocks)
    diag_all, device_pair = lax.optimization_barrier((diag_all, device_pair))
    carried_in = pass_carry(device_pair, start_pair)

    def enter_span(carried, span_items):
        total_now, state_now = span_items
        return (total_now[:, None, None] * carried + state_now, carried)

    final_state, entering = lax.scan(enter_span, carried_in, (total_all, state_all))
    off_out = jnp.einsum(
        "kin,khpn->kihp",
        c_blocks,
        entering.astype(jnp.bfloat16),
        preferred_element_type=jnp.float32,
    )
    per_head = x_blocks.reshape(blocks, length, head_count, -1)
    mixed_out = diag_all.reshape(blocks, length, head_count, -1).astype(jnp.float32)
    mixed_out = mixed_out + off_out * jnp.transpose(entry_all, (0, 2, 1))[..., None]
    mixed_out = mixed_out + skip_gain[None, None, :, None] * per_head.astype(jnp.float32)
    live_rows = live_mask.reshape(blocks, length).astype(jnp.float32)
    mixed_out = (mixed_out * live_rows[:, :, None, None]).astype(jnp.bfloat16)
    ssd_out = mixed_out.reshape(1, tokens, -1)
    token_part = jnp.dot(ssd_out[0], readout, preferred_element_type=jnp.float32)
    token_scores = lax.psum(token_part, "head")
    return (ssd_out, token_scores.reshape(1, tokens))


def solution(mesh):
    placed = (
        P("rep", "ctx", "head"),
        P("rep", "ctx", "head"),
        P("rep", "ctx", "head"),
        P("rep", "head", "ctx"),
        P("rep", "ctx"),
        P("rep", "ctx"),
        P("head"),
        P("head"),
    )
    return jax.shard_map(
        body,
        mesh=mesh,
        in_specs=placed,
        out_specs=(P("rep", "ctx", "head"), P("rep", "ctx")),
        check_vma=False,
    )
```

profile of v0, /device:TPU:2, one launch (start us, length us, event | category | flops | bytes accessed | tf_op | source)
XLA Modules:
  0.0 198.0 jit_solution(17420713588232635263)
XLA Ops:
  7.8 1.3 reduce.7
  9.7 2.4 %broadcast_select_fusion.1 = bf16[2,256,1024]{2,1,0:T(8,128)(2,1)} fusion(bf16[2,256,1024]{2,1,0:T(8,128)(2,1)} %bitcast.168, pred[2,256]{1,0:T(4,128)(4,1)S(1)} %get-tuple-element.384), kind=kLoop, calls=%fused_computation.69 | loop fusion | flops 524288 | bytes 2097664 | tf_op jit(solution)/shard_map/jit(_where)/select_n | solution.py:90
  12.2 2.3 %copy.21 = bf16[2,256,1024]{1,2,0:T(8,128)(2,1)} copy(bf16[2,256,1024]{2,1,0:T(8,128)(2,1)} %broadcast_select_fusion.1) | data formatting | bytes 2097152 | tf_op jit(solution)/shard_map/while | solution.py:72
  14.5 9.0 %while.69 = (s32[]{:T(128)}, f32[2,16,64,256]{3,2,1,0:T(8,128)S(1)}, f32[2,16]{1,0:T(2,128)S(1)}, f32[2,16,256]{2,1,0:T(8,128)S(1)}, bf16[2,256,1024]{1,2,0:T(8,...) while((s32[]{:T(128)}, ...), condition=%wide.region_3.4_spmd.clone, body=%wide.region_2.3_spmd.sunk.clone | while | flops 139408144 | bytes 3372799 | solution.py:98
  17.1 1.1 constant_dynamic-slice_fusion.10
  18.2 0.8 fusion.99
  21.6 1.1 constant_dynamic-slice_fusion.10
  22.7 0.8 fusion.99
  24.0 1.0 copy-done
  25.0 10.6 %while.68 = (s32[]{:T(128)}, bf16[2,256,1024]{1,2,0:T(8,128)(2,1)}, bf16[2,256,1024]{1,2,0:T(8,128)(2,1)}, s32[2,256]{1,0:T(2,128)S(1)}, bf16[2,16,256]{2,1,0:T(...) while((s32[]{:T(128)}, bf16[2,256,1024]{1,2,0:T(8,128)(2,1)}, ...), condition=%wide.region_1.2_spmd.clone, body=%wide.region_0.1_spmd.sunk.clone | while | flops 176488704 | bytes 12497045 | solution.py:72
  25.0 1.1 fusion.91
  26.1 1.1 constant_dynamic-slice_fusion.9
  27.7 1.6 fusion.95
  29.3 1.0 copy-done.7
  30.3 1.1 fusion.91
  31.4 1.1 constant_dynamic-slice_fusion.9
  32.9 1.6 fusion.95
  34.6 1.0 copy-done.7
  35.6 4.0 %reshape.119 = bf16[2,256,16,64]{3,2,1,0:T(8,128)(2,1)} reshape(bf16[1,512,1024]{2,1,0:T(8,128)(2,1)} %param.18) | data formatting | bytes 2097152 | tf_op jit(solution)/shard_map/squeeze | solution.py:90
  39.6 1.3 dynamic-slice
  41.8 34.5 %all-reduce = f32[256]{0:T(256)S(1)} all-reduce(f32[256]{0:T(256)S(1)} %dynamic-update-slice), channel_id=2, replica_groups=mesh['head'=8,'ctx'=16,'rep'=4] {'ctx'}, use_global_device_ids=true, to_apply=%add | all-reduce | flops 256 | bytes 2048
  76.3 3.7 %copy.26 = bf16[2,256,16,64]{1,3,2,0:T(8,128)(2,1)} copy(bf16[2,256,16,64]{3,2,1,0:T(8,128)(2,1)} %reshape.119) | data formatting | bytes 2097152 | tf_op jit(solution)/shard_map/squeeze | solution.py:90
  80.0 1.1 broadcast_convert_fusion
  81.1 58.3 %all-gather.4.cloned.1.call-done = f32[256,64,256]{2,1,0:T(8,128)} async-done(((f32[16,64,256]{2,1,0:T(8,128)}), f32[256,64,256]{2,1,0:T(8,128)}) %all-gather.4.cloned.1.call-update) | async-done | bytes 16777232 | tf_op jit(solution)/shard_map/all_gather | solution.py:12
  139.4 22.5 %while.72 = (s32[]{:T(128)}, f32[16,64,256]{2,1,0:T(8,128)S(1)}, s32[]{:T(128)}, f32[16,16]{1,0:T(8,128)S(1)}, f32[16,16,64,256]{3,2,1,0:T(8,128)}) while((s32[]{:T(128)}, f32[16,64,256]{2,1,0:T(8,128)S(1)}, s32[]{:T(128)}, f32[16,16]{1,0:T(8,128)S(1)}, f32[16,16,64,256]{3,2,1,0:T(8,128)}) %tuple.153), condition=%wide.region_7.8_spmd.clone.clone, body=%wide.region_6.7_spmd.clone.sunk.clone | while | flops 1048580 | bytes 3146009 | solution.py:21
  139.4 1.5 fusion.102
  140.9 1.5 fusion.102
  142.4 1.5 fusion.102
  143.9 1.5 fusion.102
  145.4 1.5 fusion.102
  146.9 1.5 fusion.102
  148.4 1.5 fusion.102
  149.9 1.5 fusion.102
  151.4 1.5 fusion.102
  152.9 1.5 fusion.102
  154.4 1.5 fusion.102
  155.9 1.5 fusion.102
  157.4 1.5 fusion.102
  158.9 1.5 fusion.102
  160.4 1.5 fusion.102
  161.9 2.3 %while.70 = (s32[]{:T(128)}, f32[16,64,256]{2,1,0:T(8,128)S(1)}, bf16[2,16,64,256]{3,2,1,0:T(8,128)(2,1)}, f32[2,16]{1,0:T(2,128)S(1)}, f32[2,16,64,256]{3,2,1,0:T(8,128)S(1)}) while((s32[]{:T(128)}, f32[16,64,256]{2,1,0:T(8,128)S(1)}, bf16[2,16,64,256]{3,2,1,0:T(8,128)(2,1)}, f32[2,16]{1,0:T(2,128)S(1)}, ...), condition=%wide.region_9.10_spmd.clone, body=%wide.region_8.9_spmd.sunk.clone | while | flops 524290 | bytes 5243653 | solution.py:116
  161.9 0.9 bitcast_dynamic-update-slice_fusion.7
  163.1 0.8 bitcast_dynamic-update-slice_fusion.7
  164.2 2.6 %fusion.41 = bf16[2,256,16,64]{1,3,2,0:T(8,128)(2,1)S(1)} fusion(bf16[2,256,16,64]{1,3,2,0:T(8,128)(2,1)} %bitcast.178, bf16[2,256,256,1]{2,1,3,0:T(8,128)(2,1)S(1)} %bitcast.173, f32[2,256]{1,0:T(2,128)S(1)} %get-tuple-element.385, bf16[2,256,16,64]{1,3,2,0:T(8,128)(2,1)} %copy.26, f32[16]{0:T(128)S(1)} %copy-done.8, f32[2,256,16]{1,2,0:T(8,128)S(1)} %bitcast.179, ...), kind=kOutput, calls=%fused_computation.66 | convolution fusion | flops 273154048 | bytes 4491840 | tf_op jit(solution)/shard_map/kin,khpn->kihp/dot_general | solution.py:117
  166.8 2.0 %copy.33 = bf16[2,256,16,64]{3,2,1,0:T(8,128)(2,1)S(1)} copy(bf16[2,256,16,64]{1,3,2,0:T(8,128)(2,1)S(1)} %fusion.41) | data formatting | bytes 2097152
  168.8 2.1 %copy.27 = bf16[2,256,16,64]{1,0,3,2:T(2,128)(2,1)} copy(bf16[2,256,16,64]{1,3,2,0:T(8,128)(2,1)S(1)} %fusion.41) | data formatting | bytes 2097152 | tf_op jit(solution)/shard_map/convert_element_type | solution.py:128
  170.9 2.3 %reshape.120 = bf16[1,512,1024]{2,1,0:T(8,128)(2,1)} reshape(bf16[2,256,16,64]{3,2,1,0:T(8,128)(2,1)S(1)} %copy.33) | data formatting | bytes 2097152
  173.6 17.5 %psum.7 = f32[1,512]{1,0:T(1,128)} all-reduce(f32[1,512]{1,0:T(1,128)S(1)} %fusion.45), channel_id=1, replica_groups=mesh['head'=8,'ctx'=16,'rep'=4] {'head'}, use_global_device_ids=true, to_apply=%region_10.11 | all-reduce | flops 512 | bytes 4096 | tf_op jit(solution)/shard_map/psum | solution.py:131
  (89 shorter events, 7.9 us)
Async XLA Ops:
  7.2 132.2 %all-gather.4.cloned.1.call-start = ((), (), s32[]{:S(2)}) async-start(), calls=%async_computation | async-start | bytes 17825792 | tf_op jit(solution)/shard_map/all_gather | solution.py:12
  9.7 4.7 %copy-start.4 = (bf16[1,16,512]{2,1,0:T(8,128)(2,1)S(1)}, bf16[1,16,512]{2,1,0:T(8,128)(2,1)}, u32[]{:S(2)}) copy-start(bf16[1,16,512]{2,1,0:T(8,128)(2,1)} %param.21) | copy-start | bytes 49156
  9.7 4.8 %copy-start.1 = (bf16[1,512,256]{2,1,0:T(8,128)(2,1)S(1)}, bf16[1,512,256]{2,1,0:T(8,128)(2,1)}, u32[]{:S(2)}) copy-start(bf16[1,512,256]{2,1,0:T(8,128)(2,1)} %param.19) | copy-start | bytes 786436
  24.0 1.0 copy-start
  27.7 1.6 copy-start.6
  29.3 1.0 copy-start.7
  32.9 1.6 copy-start.6
  34.6 1.0 copy-start.7
  39.6 40.4 %copy-start.5 = (bf16[1024]{0:T(1024)(128)(2,1)S(1)}, bf16[1024]{0:T(1024)(128)(2,1)}, u32[]{:S(2)}) copy-start(bf16[1024]{0:T(1024)(128)(2,1)} %param.25) | copy-start | bytes 6148
  161.9 2.3 %copy-start.3 = (bf16[2,256,256]{2,1,0:T(8,128)(2,1)S(1)}, bf16[2,256,256]{2,1,0:T(8,128)(2,1)}, u32[]{:S(2)}) copy-start(bf16[2,256,256]{2,1,0:T(8,128)(2,1)} %get-tuple-element.766) | copy-start | bytes 786436
  161.9 2.3 %copy-start.8 = (f32[16]{0:T(128)S(1)}, f32[16]{0:T(128)}, u32[]{:S(2)}) copy-start(f32[16]{0:T(128)} %param.24) | copy-start | bytes 196
  170.9 2.3 %copy-start.2 = (bf16[2,256,16,64]{1,0,3,2:T(2,128)(2,1)S(1)}, bf16[2,256,16,64]{1,0,3,2:T(2,128)(2,1)}, u32[]{:S(2)}) copy-start(bf16[2,256,16,64]{1,0,3,2:T(2,128)(2,1)} %copy.27) | copy-start | bytes 3145732
Sparse Core Ops, SparseCore 0:
  35.7 103.6 all-gather.3
where the time goes:
time: 199 us; the launch traced here: 198 us
  waiting for transfers between devices  58.3 us (29%)
  blocking collectives  52 us (26%)
  other arithmetic  29.8 us (15%)
  local copies, waits for them, and re-layouts  29.4 us (15%)
  between operations  15.5 us (8%)
  matrix products  11 us (6%)
  loops' own time  1.99 us (1%)
    all_gather x1, waiting for transfers between devices, entering_2(): pieces = jax.tree.map(lambda part: lax.all_gather(part, axis), value)  58.3 us
    unnamed x1, blocking collectives  34.5 us
    select_n x15, other arithmetic, lap(): jnp.where(position < mine, new, old)  21.9 us
    psum x1, blocking collectives, body(): token_scores = lax.psum(token_part, 'head')  17.5 us
    squeeze x2, local copies, waits for them, and re-layouts, body(): inputs[0]  7.72 us
    unnamed x22, local copies, waits for them, and re-layouts  7.55 us
    dynamic_slice x4, local copies, waits for them, and re-layouts, body(): lax.map(lambda one_span: state_part(*one_span), (x_blocks, b_blocks, a_bl...  4.33 us
  transfers between devices with their start and end apart: 1, of which 1 were waited for; matrix products, arithmetic and copies ran while one was open for 5% of the time, Pallas kernels for 0%

commit v1 on v0

--- a/solution.py
+++ b/solution.py
@@ -128,7 +128,8 @@
     mixed_out = (mixed_out * live_rows[:, :, None, None]).astype(jnp.bfloat16)
     ssd_out = mixed_out.reshape(1, tokens, -1)
     token_part = jnp.dot(ssd_out[0], readout, preferred_element_type=jnp.float32)
-    token_scores = lax.psum(token_part, "head")
+    shards = lax.all_gather(token_part, "head", axis=0, tiled=False)
+    token_scores = shards.sum(axis=0)
     return (ssd_out, token_scores.reshape(1, tokens))
 
 

time: 199 us -> 206 us (1.035)
  blocking collectives: 52 us -> 58.3 us
    all_gather x0 -> x1, blocking collectives: none -> 23.9 us  [body(): shards = lax.all_gather(token_part, 'head', axis=0, tiled=False)]
    psum x1 -> x0, blocking collectives: 17.5 us -> none  [body(): token_scores = lax.psum(token_part, 'head')]
where the time goes in v1:
time: 206 us; the launch traced here: 205 us
  waiting for transfers between devices  58.3 us (28%)
  blocking collectives  58.3 us (28%)
  other arithmetic  30.4 us (15%)
  local copies, waits for them, and re-layouts  29 us (14%)
  between operations  15.5 us (8%)
  matrix products  11 us (5%)
    all_gather x1, waiting for transfers between devices, entering_2(): pieces = jax.tree.map(lambda part: lax.all_gather(part, axis), value)  58.3 us
    unnamed x1, blocking collectives  34.5 us
    all_gather x1, blocking collectives, body(): shards = lax.all_gather(token_part, 'head', axis=0, tiled=False)  23.9 us
    select_n x15, other arithmetic, lap(): jnp.where(position < mine, new, old)  21.9 us
    squeeze x2, local copies, waits for them, and re-layouts, body(): inputs[0]  7.71 us
    unnamed x22, local copies, waits for them, and re-layouts  7.55 us
    dynamic_slice x4, local copies, waits for them, and re-layouts, body(): lax.map(lambda one_span: state_part(*one_span), (x_blocks, b_blocks, a_bl...  4.33 us
  transfers between devices with their start and end apart: 1, of which 1 were waited for; matrix products, arithmetic and copies ran while one was open for 5% of the time, Pallas kernels for 0%

profile of v1, /device:TPU:2, one launch (start us, length us, event | category | flops | bytes accessed | tf_op | source)
XLA Modules:
  0.0 204.5 jit_solution(15919704281530148364)
XLA Ops:
  7.8 1.3 reduce.8
  9.7 2.4 %broadcast_select_fusion.1 = bf16[2,256,1024]{2,1,0:T(8,128)(2,1)} fusion(bf16[2,256,1024]{2,1,0:T(8,128)(2,1)} %bitcast.172, pred[2,256]{1,0:T(4,128)(4,1)S(1)} %get-tuple-element.384), kind=kLoop, calls=%fused_computation.70 | loop fusion | flops 524288 | bytes 2097664 | tf_op jit(solution)/shard_map/jit(_where)/select_n | solution.py:90
  12.2 2.3 %copy.21 = bf16[2,256,1024]{1,2,0:T(8,128)(2,1)} copy(bf16[2,256,1024]{2,1,0:T(8,128)(2,1)} %broadcast_select_fusion.1) | data formatting | bytes 2097152 | tf_op jit(solution)/shard_map/while | solution.py:72
  14.5 9.0 %while.69 = (s32[]{:T(128)}, f32[2,16,64,256]{3,2,1,0:T(8,128)S(1)}, f32[2,16]{1,0:T(2,128)S(1)}, f32[2,16,256]{2,1,0:T(8,128)S(1)}, bf16[2,256,1024]{1,2,0:T(8,...) while((s32[]{:T(128)}, ...), condition=%wide.region_3.4_spmd.clone, body=%wide.region_2.3_spmd.sunk.clone | while | flops 139408144 | bytes 3372799 | solution.py:98
  17.1 1.1 constant_dynamic-slice_fusion.10
  18.2 0.8 fusion.98
  21.6 1.1 constant_dynamic-slice_fusion.10
  22.7 0.8 fusion.98
  24.0 1.0 copy-done
  25.0 10.2 %while.68 = (s32[]{:T(128)}, bf16[2,256,1024]{1,2,0:T(8,128)(2,1)}, bf16[2,256,1024]{1,2,0:T(8,128)(2,1)}, s32[2,256]{1,0:T(2,128)S(1)}, bf16[2,16,256]{2,1,0:T(...) while((s32[]{:T(128)}, bf16[2,256,1024]{1,2,0:T(8,128)(2,1)}, ...), condition=%wide.region_1.2_spmd.clone, body=%wide.region_0.1_spmd.sunk.clone | while | flops 176488704 | bytes 4108889 | solution.py:72
  25.0 1.1 fusion.90
  26.1 1.1 constant_dynamic-slice_fusion.9
  27.6 1.6 fusion.94
  29.2 0.8 constant_dynamic-update-slice_fusion.3
  30.1 1.1 fusion.90
  31.2 1.1 constant_dynamic-slice_fusion.9
  32.7 1.6 fusion.94
  34.3 0.8 constant_dynamic-update-slice_fusion.3
  35.2 4.0 %reshape.123 = bf16[2,256,16,64]{3,2,1,0:T(8,128)(2,1)} reshape(bf16[1,512,1024]{2,1,0:T(8,128)(2,1)} %param.18) | data formatting | bytes 2097152 | tf_op jit(solution)/shard_map/squeeze | solution.py:90
  39.2 1.3 dynamic-slice
  41.4 34.5 %all-reduce = f32[256]{0:T(256)S(1)} all-reduce(f32[256]{0:T(256)S(1)} %dynamic-update-slice), channel_id=2, replica_groups=mesh['head'=8,'ctx'=16,'rep'=4] {'ctx'}, use_global_device_ids=true, to_apply=%add | all-reduce | flops 256 | bytes 2048
  75.9 3.7 %copy.26 = bf16[2,256,16,64]{1,3,2,0:T(8,128)(2,1)} copy(bf16[2,256,16,64]{3,2,1,0:T(8,128)(2,1)} %reshape.123) | data formatting | bytes 2097152 | tf_op jit(solution)/shard_map/squeeze | solution.py:90
  79.6 1.1 broadcast_convert_fusion
  80.7 58.3 %all-gather.6.cloned.1.call-done = f32[256,64,256]{2,1,0:T(8,128)} async-done(((f32[16,64,256]{2,1,0:T(8,128)}), f32[256,64,256]{2,1,0:T(8,128)}) %all-gather.6.cloned.1.call-update) | async-done | bytes 16777232 | tf_op jit(solution)/shard_map/all_gather | solution.py:12
  139.0 22.5 %while.72 = (s32[]{:T(128)}, f32[16,64,256]{2,1,0:T(8,128)S(1)}, s32[]{:T(128)}, f32[16,16]{1,0:T(8,128)S(1)}, f32[16,16,64,256]{3,2,1,0:T(8,128)}) while((s32[]{:T(128)}, f32[16,64,256]{2,1,0:T(8,128)S(1)}, s32[]{:T(128)}, f32[16,16]{1,0:T(8,128)S(1)}, f32[16,16,64,256]{3,2,1,0:T(8,128)}) %tuple.153), condition=%wide.region_7.8_spmd.clone.clone, body=%wide.region_6.7_spmd.clone.sunk.clone | while | flops 1048580 | bytes 3146009 | solution.py:21
  139.0 1.5 fusion.101
  140.5 1.5 fusion.101
  142.0 1.5 fusion.101
  143.5 1.5 fusion.101
  145.0 1.5 fusion.101
  146.5 1.5 fusion.101
  148.0 1.5 fusion.101
  149.5 1.5 fusion.101
  151.0 1.5 fusion.101
  152.5 1.5 fusion.101
  154.0 1.5 fusion.101
  155.5 1.5 fusion.101
  157.0 1.5 fusion.101
  158.5 1.5 fusion.101
  160.0 1.5 fusion.101
  161.5 2.3 %while.70 = (s32[]{:T(128)}, f32[16,64,256]{2,1,0:T(8,128)S(1)}, bf16[2,16,64,256]{3,2,1,0:T(8,128)(2,1)}, f32[2,16]{1,0:T(2,128)S(1)}, f32[2,16,64,256]{3,2,1,0:T(8,128)S(1)}) while((s32[]{:T(128)}, f32[16,64,256]{2,1,0:T(8,128)S(1)}, bf16[2,16,64,256]{3,2,1,0:T(8,128)(2,1)}, f32[2,16]{1,0:T(2,128)S(1)}, ...), condition=%wide.region_9.10_spmd.clone, body=%wide.region_8.9_spmd.sunk.clone | while | flops 524290 | bytes 5243653 | solution.py:116
  161.5 0.9 bitcast_dynamic-update-slice_fusion.7
  162.6 0.9 bitcast_dynamic-update-slice_fusion.7
  163.8 2.6 %fusion.41 = bf16[2,256,16,64]{1,3,2,0:T(8,128)(2,1)S(1)} fusion(bf16[2,256,16,64]{1,3,2,0:T(8,128)(2,1)} %bitcast.42, bf16[2,256,256,1]{2,1,3,0:T(8,128)(2,1)S(1)} %bitcast.177, f32[2,256]{1,0:T(2,128)S(1)} %get-tuple-element.385, bf16[2,256,16,64]{1,3,2,0:T(8,128)(2,1)} %copy.26, f32[16]{0:T(128)S(1)} %copy-done.6, f32[2,256,16]{1,2,0:T(8,128)S(1)} %bitcast.183, ...), kind=kOutput, calls=%fused_computation.66 | convolution fusion | flops 273154048 | bytes 4491840 | tf_op jit(solution)/shard_map/kin,khpn->kihp/dot_general | solution.py:117
  166.4 2.0 copy.33
  168.4 2.1 %copy.27 = bf16[2,256,16,64]{1,0,3,2:T(2,128)(2,1)} copy(bf16[2,256,16,64]{1,3,2,0:T(8,128)(2,1)S(1)} %fusion.41) | data formatting | bytes 2097152 | tf_op jit(solution)/shard_map/convert_element_type | solution.py:128
  170.5 2.3 %reshape.124 = bf16[1,512,1024]{2,1,0:T(8,128)(2,1)} reshape(bf16[2,256,16,64]{3,2,1,0:T(8,128)(2,1)S(1)} %copy.33) | data formatting | bytes 2097152
  173.2 23.9 %all-gather.3 = f32[8,1,512]{2,1,0:T(1,128)S(1)} all-gather(f32[1,1,512]{2,1,0:T(1,128)S(1)} %convolution_bitcast_fusion), channel_id=4, replica_groups=mesh['head'=8,'ctx'=16,'rep'=4] {'head'}, dimensions={0}, use_global_device_ids=true | all-gather | bytes 18432 | tf_op jit(solution)/shard_map/all_gather | solution.py:131
  (82 shorter events, 8.4 us)
Async XLA Ops:
  7.2 131.8 %all-gather.6.cloned.1.call-start = ((), (), s32[]{:S(2)}) async-start(), calls=%async_computation | async-start | bytes 17825792 | tf_op jit(solution)/shard_map/all_gather | solution.py:12
  9.7 4.7 %copy-start.4 = (bf16[1,16,512]{2,1,0:T(8,128)(2,1)S(1)}, bf16[1,16,512]{2,1,0:T(8,128)(2,1)}, u32[]{:S(2)}) copy-start(bf16[1,16,512]{2,1,0:T(8,128)(2,1)} %param.21) | copy-start | bytes 49156
  9.7 4.8 %copy-start.1 = (bf16[1,512,256]{2,1,0:T(8,128)(2,1)S(1)}, bf16[1,512,256]{2,1,0:T(8,128)(2,1)}, u32[]{:S(2)}) copy-start(bf16[1,512,256]{2,1,0:T(8,128)(2,1)} %param.19) | copy-start | bytes 786436
  24.0 1.0 copy-start
  39.2 40.4 %copy-start.5 = (bf16[1024]{0:T(1024)(128)(2,1)S(1)}, bf16[1024]{0:T(1024)(128)(2,1)}, u32[]{:S(2)}) copy-start(bf16[1024]{0:T(1024)(128)(2,1)} %param.25) | copy-start | bytes 6148
  161.5 2.3 %copy-start.3 = (bf16[2,256,256]{2,1,0:T(8,128)(2,1)S(1)}, bf16[2,256,256]{2,1,0:T(8,128)(2,1)}, u32[]{:S(2)}) copy-start(bf16[2,256,256]{2,1,0:T(8,128)(2,1)} %get-tuple-element.766) | copy-start | bytes 786436
  161.5 2.3 %copy-start.6 = (f32[16]{0:T(128)S(1)}, f32[16]{0:T(128)}, u32[]{:S(2)}) copy-start(f32[16]{0:T(128)} %param.24) | copy-start | bytes 196
  170.5 2.3 %copy-start.2 = (bf16[2,256,16,64]{1,0,3,2:T(2,128)(2,1)S(1)}, bf16[2,256,16,64]{1,0,3,2:T(2,128)(2,1)}, u32[]{:S(2)}) copy-start(bf16[2,256,16,64]{1,0,3,2:T(2,128)(2,1)} %copy.27) | copy-start | bytes 3145732
Sparse Core Ops, SparseCore 0:
  35.3 103.6 all-gather.5
